TPU v7x, 32 devices: a whole 2x2x4 slice. The times are simulated.
32 devices in a mesh: atoms: 8 (over z, y), waves: 4 (over x, core).
Axes of the slice: x: 2, y: 2, z: 4, core: 2. Of those that a mesh axis runs over, the one named last changes fastest.
Arguments:
- features: bfloat16 [2048, 512], P('atoms'), may hold values from -6 to 6
- positions: int32 [3, 2048], P(None, 'atoms'), may hold values from 0 to 65535
- neighbours: int32 [16, 12], P('atoms'), may hold values from 0 to 15, as said below
- wavevectors: int32 [3, 4096], P(None, 'waves'), may hold values from -16 to 16
- radial_width: float32 [8], P('waves'), may hold values from 0.05 to 0.3
- short_weight: bfloat16 [8, 512, 512], P('waves'), may hold values from -0.09375 to 0.09375
- latent_weight: bfloat16 [512, 256], replicated, may hold values from -0.25 to 0.25
- mix_weight: float32 [256, 256], replicated, may hold values from -0.375 to 0.375
- filter_rate: float32 [256], replicated, may hold values from 0.0005 to 0.02
- out_weight: bfloat16 [256, 512], replicated, may hold values from -0.375 to 0.375
Outputs:
- message: bfloat16 [2048, 512], P('atoms', 'waves')
Inputs may be any that keep to these rules, and one draw needn't show every extreme that they name: `neighbours`: row b holds 12 different block numbers, each within 7 blocks of b counted cyclically over the 16 blocks; b itself may appear.
All inputs are finite; a program needn't handle non-finite values.
Results may differ from a plain program's by a relative error of at most 0.012.
Values may be sent and summed in bfloat16 or wider, within the bound.
A program may use at most 64 MiB of HBM per device.

v0:
```python
import math

import jax
import jax.numpy as jnp
from jax import lax
from jax.sharding import PartitionSpec as P

K = 4096
RADIAL = 8
BLOCK = 128
NBR = 12
REACH = 7


cutoff = 0.5


def shifted(value, axis, steps):
    count = lax.axis_size(axis)
    pairs = [(source, (source + steps) % count) for source in range(count)]
    return lax.ppermute(value, axis, pairs)


def kernels(own_pos, near_pos, centers, radial_width):
    offsets = own_pos[:, None, :, None] - near_pos[:, :, None, :]
    offsets = jnp.mod(offsets, 65536)
    offsets = jnp.where(offsets >= 32768, offsets - 65536, offsets)
    coords = offsets.astype(jnp.float32) * (1.0 / 65536.0)
    dist_sq = jnp.sum(coords * coords, axis=0)
    distance = jnp.sqrt(dist_sq)
    smooth = jnp.where(
        dist_sq < cutoff * cutoff, jnp.square(1.0 - dist_sq / (cutoff * cutoff)), 0.0
    )
    shaped = (distance[None] - centers[:, None, None, None]) / radial_width[:, None, None, None]
    norm_scale = 1.0 / math.sqrt(NBR * BLOCK)
    return (jnp.exp(-jnp.square(shaped)) * smooth[None] * norm_scale).astype(jnp.bfloat16)


def phases_of(wavevectors, spots):
    phase_turn = (
        wavevectors[0][:, None] * spots[0][None, :]
        + wavevectors[1][:, None] * spots[1][None, :]
        + wavevectors[2][:, None] * spots[2][None, :]
    )
    phase_turn = jnp.mod(phase_turn, 65536)
    angles = phase_turn.astype(jnp.float32) * (2.0 * math.pi / 65536.0)
    return jnp.concatenate([jnp.cos(angles), jnp.sin(angles)], axis=0).astype(jnp.bfloat16)


def filter_gain(wavevectors, filter_rate):
    lengths = jnp.sum(wavevectors * wavevectors, axis=0).astype(jnp.float32)
    return jnp.exp(-lengths[:, None] * filter_rate[None, :])


def local(
    features,
    positions,
    neighbours,
    wavevectors,
    radial_width,
    short_weight,
    latent_weight,
    mix_weight,
    filter_rate,
    out_weight,
):
    row_count = features.shape[0]
    channels = features.shape[1]
    blocks_here = row_count // BLOCK
    atom_devices = lax.axis_size("atoms")
    total_blocks = blocks_here * atom_devices
    reach_hops = -(-REACH // blocks_here)
    window_feat = []
    window_pos = []
    for offset in range(-reach_hops, reach_hops + 1):
        if offset == 0:
            arrived = (features, positions)
        else:
            arrived = shifted((features, positions), "atoms", -offset)
        window_feat.append(arrived[0])
        window_pos.append(arrived[1])
    window_feat = jnp.concatenate(window_feat, axis=0).reshape(-1, BLOCK, channels)
    window_pos = jnp.concatenate(window_pos, axis=1).reshape(3, -1, BLOCK)
    first_block = lax.axis_index("atoms") * blocks_here - reach_hops * blocks_here
    local_near = jnp.mod(neighbours - first_block, total_blocks)
    own_pos = positions.reshape(3, blocks_here, BLOCK)
    local_kernels = radial_width.shape[0]
    kernel_ids = lax.axis_index("waves") * local_kernels + jnp.arange(
        local_kernels, dtype=jnp.int32
    )
    centers = cutoff * kernel_ids.astype(jnp.float32) / (RADIAL - 1)
    flat_weight = short_weight.reshape(local_kernels * channels, channels)

    def short_block(block_index):
        near_blocks = local_near[block_index]
        near_feat = window_feat[near_blocks]
        near_pos = window_pos[:, near_blocks]
        weights = kernels(own_pos[:, block_index], near_pos, centers, radial_width)
        gathered = jnp.einsum(
            "rjia,jac->irc", weights, near_feat, preferred_element_type=jnp.float32
        )
        gathered = gathered.astype(jnp.bfloat16).reshape(BLOCK, local_kernels * channels)
        return jnp.dot(gathered, flat_weight, preferred_element_type=jnp.float32)

    short_range = lax.map(short_block, jnp.arange(blocks_here, dtype=jnp.int32)).reshape(
        row_count, channels
    )
    latent = jnp.dot(features, latent_weight, preferred_element_type=jnp.float32).astype(
        jnp.bfloat16
    )
    phases = phases_of(wavevectors, positions)
    partial_factors = jnp.dot(phases, latent, preferred_element_type=jnp.float32)
    gain = filter_gain(wavevectors, filter_rate)
    gain = jnp.concatenate([gain, gain], axis=0)
    norm_scale = 1.0 / math.sqrt(row_count * atom_devices)
    factors = lax.psum(partial_factors, "atoms")
    mixed = jnp.dot(factors, mix_weight, precision=lax.Precision.HIGHEST)
    filtered = (gain * mixed * norm_scale).astype(jnp.bfloat16)
    summed = lax.dot_general(
        phases, filtered, (((0,), (0,)), ((), ())), preferred_element_type=jnp.float32
    )
    summed = (summed * (1.0 / math.sqrt(K))).astype(jnp.bfloat16)
    long_range = jnp.dot(summed, out_weight, preferred_element_type=jnp.float32)
    combined = lax.psum_scatter(
        (short_range + long_range).astype(jnp.bfloat16), "waves", scatter_dimension=1, tiled=True
    )
    return combined


def solution(mesh):
    placed = (
        P("atoms", None),
        P(None, "atoms"),
        P("atoms", None),
        P(None, "waves"),
        P("waves"),
        P("waves", None, None),
        P(),
        P(),
        P(),
        P(),
    )
    return jax.shard_map(
        local, mesh=mesh, in_specs=placed, out_specs=P("atoms", "waves"), check_vma=False
    )
```

profile of v0, /device:TPU:1, one launch (start us, length us, event | category | flops | bytes accessed | tf_op | source)
XLA Modules:
  0.0 187.0 jit_solution(414027124413842475)
XLA Ops:
  6.5 3.1 %collective-permute-start = (bf16[256,512]{1,0:T(8,128)(2,1)}, bf16[256,512]{1,0:T(8,128)(2,1)S(1)}, u32[]{:S(2)}, u32[]{:S(2)}) collective-permute-start(bf16[256,512]{1,0:T(8,128)(2,1)} %param.12), channel_id=1, source_target_pairs={{0,16},{4,20},{8,24},{12,28},{16,0},{20,4},{24,8},{28,12},{1,17},{... | collective-permute-start | bytes 786440 | tf_op jit(solution)/shard_map/ppermute | solution.py:21
  9.7 2.3 %collective-permute-start.1 = (bf16[256,512]{1,0:T(8,128)(2,1)}, bf16[256,512]{1,0:T(8,128)(2,1)S(1)}, u32[]{:S(2)}, u32[]{:S(2)}) collective-permute-start(bf16[256,512]{1,0:T(8,128)(2,1)} %param.12), channel_id=1, source_target_pairs={{0,12},{4,16},{8,20},{12,24},{16,28},{20,0},{24,4},{28,8},{1,13},{... | collective-permute-start | bytes 786440 | tf_op jit(solution)/shard_map/ppermute | solution.py:21
  12.2 2.3 %collective-permute-start.7 = (s32[3,256]{1,0:T(4,128)}, s32[3,256]{1,0:T(4,128)S(1)}, u32[]{:S(2)}, u32[]{:S(2)}) collective-permute-start(s32[3,256]{1,0:T(4,128)} %param.13), channel_id=1, source_target_pairs={{0,16},{4,20},{8,24},{12,28},{16,0},{20,4},{24,8},{28,12},{1,17},{... | collective-permute-start | bytes 9224 | tf_op jit(solution)/shard_map/ppermute | solution.py:21
  16.2 4.8 %cosine_convert_fusion = (bf16[1024,256]{1,0:T(8,128)(2,1)S(1)}, bf16[1024,256]{1,0:T(8,128)(2,1)S(1)}) fusion(s32[256]{0:T(256)S(1)} %bitcast.86, s32[1024]{0:T(1024)S(1)} %bitcast.84, s32[256]{0:T(256)S(1)} %bitcast.87, s32[1024]{0:T(1024)S(1)} %bitcast.83, s32[256]{0:T(256)S(1)} %bitcast.85, s32[1024]{0:T(1024)S(1)} %bitcast.82), kind=kLoop, calls=%fused_computation.53 | loop fusion | flops 5242880 | bytes 1063936 | tf_op jit(solution)/shard_map/convert
  21.0 3.3 %fusion.28 = f32[2048,256]{1,0:T(8,128)} fusion(bf16[256,512]{1,0:T(8,128)(2,1)} %param.12, bf16[512,256]{1,0:T(8,128)(2,1)S(1)} %copy-done, bf16[1024,256]{1,0:T(8,128)(2,1)S(1)} %get-tuple-element.182, bf16[1024,256]{1,0:T(8,128)(2,1)S(1)} %get-tuple-element.181), kind=kOutput, calls=%fused_computation.46 | convolution fusion | flops 337707008 | bytes 3670016 | tf_op jit(solution)/shard_map/dot_general | solution.py:112
  25.6 7.3 %collective-permute-done.7 = s32[3,256]{1,0:T(4,128)S(1)} collective-permute-done((s32[3,256]{1,0:T(4,128)}, s32[3,256]{1,0:T(4,128)S(1)}, u32[]{:S(2)}, u32[]{:S(2)}) %collective-permute-start.7) | collective-permute-done | bytes 3104 | tf_op jit(solution)/shard_map/ppermute | solution.py:21
  32.9 36.0 %collective-permute-start.8 = (s32[3,256]{1,0:T(4,128)S(1)}, s32[3,256]{1,0:T(4,128)S(1)}, u32[]{:S(2)}, u32[]{:S(2)}) collective-permute-start(s32[3,256]{1,0:T(4,128)S(1)} %copy-done.6), channel_id=1, source_target_pairs={{0,12},{4,16},{8,20},{12,24},{16,28},{20,0},{24,4},{28,8},{1,13},{... | collective-permute-start | bytes 9224 | tf_op jit(solution)/shard_map/ppermute | solution.py:21
  69.7 3.0 %collective-permute-start.9 = (s32[3,256]{1,0:T(4,128)S(1)}, s32[3,256]{1,0:T(4,128)S(1)}, u32[]{:S(2)}, u32[]{:S(2)}) collective-permute-start(s32[3,256]{1,0:T(4,128)S(1)} %copy-done.6), channel_id=1, source_target_pairs={{0,8},{4,12},{8,16},{12,20},{16,24},{20,28},{24,0},{28,4},{1,9},{5... | collective-permute-start | bytes 9224 | tf_op jit(solution)/shard_map/ppermute | solution.py:21
  74.0 2.1 %collective-permute-start.10 = (s32[3,256]{1,0:T(4,128)S(1)}, s32[3,256]{1,0:T(4,128)S(1)}, u32[]{:S(2)}, u32[]{:S(2)}) collective-permute-start(s32[3,256]{1,0:T(4,128)S(1)} %copy-done.6), channel_id=1, source_target_pairs={{0,4},{4,8},{8,12},{12,16},{16,20},{20,24},{24,28},{28,0},{1,5},{5... | collective-permute-start | bytes 9224 | tf_op jit(solution)/shard_map/ppermute | solution.py:21
  76.1 3.1 %collective-permute-done.10 = s32[3,256]{1,0:T(4,128)S(1)} collective-permute-done((s32[3,256]{1,0:T(4,128)S(1)}, s32[3,256]{1,0:T(4,128)S(1)}, u32[]{:S(2)}, u32[]{:S(2)}) %collective-permute-start.10) | collective-permute-done | bytes 3104 | tf_op jit(solution)/shard_map/ppermute | solution.py:21
  80.1 1.8 collective-permute-done.11
  82.1 2.4 %collective-permute-done.12 = s32[3,256]{1,0:T(4,128)S(1)} collective-permute-done((s32[3,256]{1,0:T(4,128)S(1)}, s32[3,256]{1,0:T(4,128)S(1)}, u32[]{:S(2)}, u32[]{:S(2)}) %collective-permute-start.12) | collective-permute-done | bytes 3104 | tf_op jit(solution)/shard_map/ppermute | solution.py:21
  84.4 2.5 %collective-permute-start.13 = (s32[3,256]{1,0:T(4,128)S(1)}, s32[3,256]{1,0:T(4,128)S(1)}, u32[]{:S(2)}, u32[]{:S(2)}) collective-permute-start(s32[3,256]{1,0:T(4,128)S(1)} %copy-done.6), channel_id=1, source_target_pairs={{0,20},{4,24},{8,28},{12,0},{16,4},{20,8},{24,12},{28,16},{1,21},{... | collective-permute-start | bytes 9224 | tf_op jit(solution)/shard_map/ppermute | solution.py:21
  88.1 6.0 %collective-permute-start.4 = (bf16[256,512]{1,0:T(8,128)(2,1)S(1)}, bf16[256,512]{1,0:T(8,128)(2,1)S(1)}, u32[]{:S(2)}, u32[]{:S(2)}) collective-permute-start(bf16[256,512]{1,0:T(8,128)(2,1)S(1)} %copy-done.5), channel_id=1, source_target_pairs={{0,28},{4,0},{8,4},{12,8},{16,12},{20,16},{24,20},{28,24},{1,29},{... | collective-permute-start | bytes 786440 | tf_op jit(solution)/shard_map/ppermute | solution.py:21
  94.4 5.6 %collective-permute-done.4 = bf16[256,512]{1,0:T(8,128)(2,1)S(1)} collective-permute-done((bf16[256,512]{1,0:T(8,128)(2,1)S(1)}, bf16[256,512]{1,0:T(8,128)(2,1)S(1)}, u32[]{:S(2)}, u32[]{:S(2)}) %collective-permute-start.4) | collective-permute-done | bytes 262176 | tf_op jit(solution)/shard_map/ppermute | solution.py:21
  100.1 7.6 %collective-permute-done.5 = bf16[256,512]{1,0:T(8,128)(2,1)S(1)} collective-permute-done((bf16[256,512]{1,0:T(8,128)(2,1)S(1)}, bf16[256,512]{1,0:T(8,128)(2,1)S(1)}, u32[]{:S(2)}, u32[]{:S(2)}) %collective-permute-start.5) | collective-permute-done | bytes 262176 | tf_op jit(solution)/shard_map/ppermute | solution.py:21
  107.6 4.6 %collective-permute-done.6 = bf16[256,512]{1,0:T(8,128)(2,1)S(1)} collective-permute-done((bf16[256,512]{1,0:T(8,128)(2,1)S(1)}, bf16[256,512]{1,0:T(8,128)(2,1)S(1)}, u32[]{:S(2)}, u32[]{:S(2)}) %collective-permute-start.6) | collective-permute-done | bytes 262176 | tf_op jit(solution)/shard_map/ppermute | solution.py:21
  113.7 18.6 %while.13 = (s32[]{:T(128)}, f32[2,128,512]{2,1,0:T(8,128)}, s32[2]{0:T(128)S(1)}, s32[2,12]{1,0:T(2,128)S(1)}, bf16[18,128,512]{2,1,0:T(8,128)(2,1)}, /*index=5...) while((s32[]{:T(128)}, f32[2,128,512]{2,1,0:T(8,128)}, ...), condition=%wide.region_2.3_spmd.clone, body=%wide.region_0.2_spmd.clone.sunk | while | flops 551748608 | bytes 15567875 | solution.py:105
  115.9 2.3 %gather_fusion = bf16[12,128,512]{2,1,0:T(8,128)(2,1)S(1)} fusion(bf16[18,128,512]{2,1,0:T(8,128)(2,1)} %get-tuple-element.281, s32[1024]{0:T(1024)S(1)} %pad_clamp_fusion.2), kind=kCustom, calls=%fused_computation.clone.clone.1 | custom fusion | bytes 3145776 | tf_op jit(solution)/shard_map/while/body/eval_jaxpr/gather | solution.py:96
  125.2 2.3 %gather_fusion = bf16[12,128,512]{2,1,0:T(8,128)(2,1)S(1)} fusion(bf16[18,128,512]{2,1,0:T(8,128)(2,1)} %get-tuple-element.281, s32[1024]{0:T(1024)S(1)} %pad_clamp_fusion.2), kind=kCustom, calls=%fused_computation.clone.clone.1 | custom fusion | bytes 3145776 | tf_op jit(solution)/shard_map/while/body/eval_jaxpr/gather | solution.py:96
  132.3 21.0 %all-reduce.2.cloned.1.call-done = f32[2048,256]{1,0:T(8,128)} async-done(((f32[2048,256]{1,0:T(8,128)}), f32[2048,256]{1,0:T(8,128)}) %all-reduce.2.cloned.1.call-update) | async-done | bytes 2097168 | tf_op jit(solution)/shard_map/psum | solution.py:116
  153.2 4.1 %fusion.25 = bf16[2048,256]{1,0:T(8,128)(2,1)S(1)} fusion(f32[2048,256]{1,0:T(8,128)} %all-reduce.2.cloned.1.call-done, f32[256,256]{1,0:T(8,128)} %param.19, f32[1024,256]{1,0:T(8,128)} %multiply_exponential_fusion), kind=kOutput, calls=%fused_computation.37 | convolution fusion | flops 1612709888 | bytes 4456448 | tf_op jit(solution)/shard_map/dot_general | solution.py:117
  158.9 19.7 %reduce-scatter.4.cloned.1.call-done = bf16[128,256]{1,0:T(8,128)(2,1)} async-done(((bf16[512,256]{1,0:T(8,128)(2,1)}), bf16[128,256]{1,0:T(8,128)(2,1)}) %reduce-scatter.4.cloned.1.call-update) | async-done | bytes 65552
  178.6 1.6 copy.22
  (101 shorter events, 21.1 us)
Async XLA Ops:
  6.5 14.4 %copy-start = (bf16[512,256]{1,0:T(8,128)(2,1)S(1)}, bf16[512,256]{1,0:T(8,128)(2,1)}, u32[]{:S(2)}) copy-start(bf16[512,256]{1,0:T(8,128)(2,1)} %param.18) | copy-start | bytes 786436
  6.5 146.7 %all-reduce.2.cloned.1.call-start = ((), (), s32[]{:S(2)}) async-start(), calls=%async_computation.1 | async-start | bytes 4194304 | tf_op jit(solution)/shard_map/psum | solution.py:116
  6.5 87.6 %collective-permute-start = (bf16[256,512]{1,0:T(8,128)(2,1)}, bf16[256,512]{1,0:T(8,128)(2,1)S(1)}, u32[]{:S(2)}, u32[]{:S(2)}) collective-permute-start(bf16[256,512]{1,0:T(8,128)(2,1)} %param.12), channel_id=1, source_target_pairs={{0,16},{4,20},{8,24},{12,28},{16,0},{20,4},{24,8},{28,12},{1,17},{... | collective-permute-start | bytes 786440 | tf_op jit(solution)/shard_map/ppermute | solution.py:21
  9.7 84.6 %collective-permute-start.1 = (bf16[256,512]{1,0:T(8,128)(2,1)}, bf16[256,512]{1,0:T(8,128)(2,1)S(1)}, u32[]{:S(2)}, u32[]{:S(2)}) collective-permute-start(bf16[256,512]{1,0:T(8,128)(2,1)} %param.12), channel_id=1, source_target_pairs={{0,12},{4,16},{8,20},{12,24},{16,28},{20,0},{24,4},{28,8},{1,13},{... | collective-permute-start | bytes 786440 | tf_op jit(solution)/shard_map/ppermute | solution.py:21
  11.9 82.4 %collective-permute-start.2 = (bf16[256,512]{1,0:T(8,128)(2,1)}, bf16[256,512]{1,0:T(8,128)(2,1)S(1)}, u32[]{:S(2)}, u32[]{:S(2)}) collective-permute-start(bf16[256,512]{1,0:T(8,128)(2,1)} %param.12), channel_id=1, source_target_pairs={{0,8},{4,12},{8,16},{12,20},{16,24},{20,28},{24,0},{28,4},{1,9},{5... | collective-permute-start | bytes 786440 | tf_op jit(solution)/shard_map/ppermute | solution.py:21
  11.9 82.4 %collective-permute-start.3 = (bf16[256,512]{1,0:T(8,128)(2,1)}, bf16[256,512]{1,0:T(8,128)(2,1)S(1)}, u32[]{:S(2)}, u32[]{:S(2)}) collective-permute-start(bf16[256,512]{1,0:T(8,128)(2,1)} %param.12), channel_id=1, source_target_pairs={{0,4},{4,8},{8,12},{12,16},{16,20},{20,24},{24,28},{28,0},{1,5},{5... | collective-permute-start | bytes 786440 | tf_op jit(solution)/shard_map/ppermute | solution.py:21
  12.2 20.7 %collective-permute-start.7 = (s32[3,256]{1,0:T(4,128)}, s32[3,256]{1,0:T(4,128)S(1)}, u32[]{:S(2)}, u32[]{:S(2)}) collective-permute-start(s32[3,256]{1,0:T(4,128)} %param.13), channel_id=1, source_target_pairs={{0,16},{4,20},{8,24},{12,28},{16,0},{20,4},{24,8},{28,12},{1,17},{... | collective-permute-start | bytes 9224 | tf_op jit(solution)/shard_map/ppermute | solution.py:21
  24.2 8.7 %copy-start.6 = (s32[3,256]{1,0:T(4,128)S(1)}, s32[3,256]{1,0:T(4,128)}, u32[]{:S(2)}) copy-start(s32[3,256]{1,0:T(4,128)} %param.13) | copy-start | bytes 9220
  24.2 63.8 %copy-start.5 = (bf16[256,512]{1,0:T(8,128)(2,1)S(1)}, bf16[256,512]{1,0:T(8,128)(2,1)}, u32[]{:S(2)}) copy-start(bf16[256,512]{1,0:T(8,128)(2,1)} %param.12) | copy-start | bytes 786436
  24.3 154.3 %reduce-scatter.4.cloned.1.call-start = ((), (), s32[]{:S(2)}) async-start(), calls=%async_computation.2 | async-start | bytes 327680
  32.9 36.8 %collective-permute-start.8 = (s32[3,256]{1,0:T(4,128)S(1)}, s32[3,256]{1,0:T(4,128)S(1)}, u32[]{:S(2)}, u32[]{:S(2)}) collective-permute-start(s32[3,256]{1,0:T(4,128)S(1)} %copy-done.6), channel_id=1, source_target_pairs={{0,12},{4,16},{8,20},{12,24},{16,28},{20,0},{24,4},{28,8},{1,13},{... | collective-permute-start | bytes 9224 | tf_op jit(solution)/shard_map/ppermute | solution.py:21
  69.7 4.3 %collective-permute-start.9 = (s32[3,256]{1,0:T(4,128)S(1)}, s32[3,256]{1,0:T(4,128)S(1)}, u32[]{:S(2)}, u32[]{:S(2)}) collective-permute-start(s32[3,256]{1,0:T(4,128)S(1)} %copy-done.6), channel_id=1, source_target_pairs={{0,8},{4,12},{8,16},{12,20},{16,24},{20,28},{24,0},{28,4},{1,9},{5... | collective-permute-start | bytes 9224 | tf_op jit(solution)/shard_map/ppermute | solution.py:21
  74.0 5.3 %collective-permute-start.10 = (s32[3,256]{1,0:T(4,128)S(1)}, s32[3,256]{1,0:T(4,128)S(1)}, u32[]{:S(2)}, u32[]{:S(2)}) collective-permute-start(s32[3,256]{1,0:T(4,128)S(1)} %copy-done.6), channel_id=1, source_target_pairs={{0,4},{4,8},{8,12},{12,16},{16,20},{20,24},{24,28},{28,0},{1,5},{5... | collective-permute-start | bytes 9224 | tf_op jit(solution)/shard_map/ppermute | solution.py:21
  79.2 2.8 %collective-permute-start.11 = (s32[3,256]{1,0:T(4,128)S(1)}, s32[3,256]{1,0:T(4,128)S(1)}, u32[]{:S(2)}, u32[]{:S(2)}) collective-permute-start(s32[3,256]{1,0:T(4,128)S(1)} %copy-done.6), channel_id=1, source_target_pairs={{0,28},{4,0},{8,4},{12,8},{16,12},{20,16},{24,20},{28,24},{1,29},{... | collective-permute-start | bytes 9224 | tf_op jit(solution)/shard_map/ppermute | solution.py:21
  82.0 2.5 %collective-permute-start.12 = (s32[3,256]{1,0:T(4,128)S(1)}, s32[3,256]{1,0:T(4,128)S(1)}, u32[]{:S(2)}, u32[]{:S(2)}) collective-permute-start(s32[3,256]{1,0:T(4,128)S(1)} %copy-done.6), channel_id=1, source_target_pairs={{0,24},{4,28},{8,0},{12,4},{16,8},{20,12},{24,16},{28,20},{1,25},{... | collective-permute-start | bytes 9224 | tf_op jit(solution)/shard_map/ppermute | solution.py:21
  84.4 3.6 %collective-permute-start.13 = (s32[3,256]{1,0:T(4,128)S(1)}, s32[3,256]{1,0:T(4,128)S(1)}, u32[]{:S(2)}, u32[]{:S(2)}) collective-permute-start(s32[3,256]{1,0:T(4,128)S(1)} %copy-done.6), channel_id=1, source_target_pairs={{0,20},{4,24},{8,28},{12,0},{16,4},{20,8},{24,12},{28,16},{1,21},{... | collective-permute-start | bytes 9224 | tf_op jit(solution)/shard_map/ppermute | solution.py:21
  88.1 12.0 %collective-permute-start.4 = (bf16[256,512]{1,0:T(8,128)(2,1)S(1)}, bf16[256,512]{1,0:T(8,128)(2,1)S(1)}, u32[]{:S(2)}, u32[]{:S(2)}) collective-permute-start(bf16[256,512]{1,0:T(8,128)(2,1)S(1)} %copy-done.5), channel_id=1, source_target_pairs={{0,28},{4,0},{8,4},{12,8},{16,12},{20,16},{24,20},{28,24},{1,29},{... | collective-permute-start | bytes 786440 | tf_op jit(solution)/shard_map/ppermute | solution.py:21
  94.1 19.6 %copy-start.2 = (bf16[2,512,512]{2,1,0:T(8,128)(2,1)S(1)}, bf16[2,512,512]{2,1,0:T(8,128)(2,1)}, u32[]{:S(2)}) copy-start(bf16[2,512,512]{2,1,0:T(8,128)(2,1)} %param.17) | copy-start | bytes 3145732
  94.1 19.6 %copy-start.14 = (f32[2]{0:T(128)S(1)}, f32[2]{0:T(128)}, u32[]{:S(2)}) copy-start(f32[2]{0:T(128)} %param.16) | copy-start | bytes 28
  94.1 13.5 %collective-permute-start.5 = (bf16[256,512]{1,0:T(8,128)(2,1)S(1)}, bf16[256,512]{1,0:T(8,128)(2,1)S(1)}, u32[]{:S(2)}, u32[]{:S(2)}) collective-permute-start(bf16[256,512]{1,0:T(8,128)(2,1)S(1)} %copy-done.5), channel_id=1, source_target_pairs={{0,24},{4,28},{8,0},{12,4},{16,8},{20,12},{24,16},{28,20},{1,25},{... | collective-permute-start | bytes 786440 | tf_op jit(solution)/shard_map/ppermute | solution.py:21
  94.2 18.0 %collective-permute-start.6 = (bf16[256,512]{1,0:T(8,128)(2,1)S(1)}, bf16[256,512]{1,0:T(8,128)(2,1)S(1)}, u32[]{:S(2)}, u32[]{:S(2)}) collective-permute-start(bf16[256,512]{1,0:T(8,128)(2,1)S(1)} %copy-done.5), channel_id=1, source_target_pairs={{0,20},{4,24},{8,28},{12,0},{16,4},{20,8},{24,12},{28,16},{1,21},{... | collective-permute-start | bytes 786440 | tf_op jit(solution)/shard_map/ppermute | solution.py:21
  132.2 25.0 %copy-start.4 = (bf16[1024,256]{1,0:T(8,128)(2,1)S(1)}, bf16[1024,256]{1,0:T(8,128)(2,1)}, u32[]{:S(2)}) copy-start(bf16[1024,256]{1,0:T(8,128)(2,1)} %copy-done.3) | copy-start | bytes 1572868
  132.2 25.0 %copy-start.12 = (f32[2,128,512]{2,1,0:T(8,128)S(1)}, f32[2,128,512]{2,1,0:T(8,128)}, u32[]{:S(2)}) copy-start(f32[2,128,512]{2,1,0:T(8,128)} %get-tuple-element.132) | copy-start | bytes 1572868
  132.2 25.1 %copy-start.13 = (bf16[256,512]{1,0:T(8,128)(2,1)S(1)}, bf16[256,512]{1,0:T(8,128)(2,1)}, u32[]{:S(2)}) copy-start(bf16[256,512]{1,0:T(8,128)(2,1)} %param.21) | copy-start | bytes 786436
  (9 other events, 16.7 us)
Sparse Core Ops, SparseCore 0:
  24.4 128.7 all-reduce.1
  159.0 19.4 reduce-scatter.3
where the time goes:
time: 188 us; the launch traced here: 187 us
  waiting for transfers between devices  76.1 us (40%)
  starting transfers between devices  58.9 us (31%)
  local copies, waits for them, and re-layouts  14.8 us (8%)
  between operations  13.7 us (7%)
  matrix products  10.3 us (5%)
  other arithmetic  9.75 us (5%)
  loops' own time  3.46 us (2%)
    ppermute x14, starting transfers between devices, shifted(): return lax.ppermute(value, axis, pairs)  58.8 us
    ppermute x14, waiting for transfers between devices, shifted(): return lax.ppermute(value, axis, pairs)  35.4 us
    psum x1, waiting for transfers between devices, local(): factors = lax.psum(partial_factors, 'atoms')  21 us
    unnamed x3, waiting for transfers between devices  19.7 us
    another operation x1, other arithmetic  4.75 us
    gather x2, local copies, waits for them, and re-layouts, short_block(): near_feat = window_feat[near_blocks]  4.64 us
    unnamed x44, local copies, waits for them, and re-layouts  4.1 us
    dot_general x1, matrix products, local(): mixed = jnp.dot(factors, mix_weight, precision=lax.Precision.HIGHEST)  4.06 us
  transfers between devices with their start and end apart: 16, of which 12 were waited for; matrix products, arithmetic and copies ran while one was open for 13% of the time, Pallas kernels for 0%

commit v1 on v0

--- a/solution.py
+++ b/solution.py
@@ -1,8 +1,11 @@
+import functools
 import math
 
 import jax
 import jax.numpy as jnp
 from jax import lax
+from jax.experimental import pallas as pl
+from jax.experimental.pallas import tpu as pltpu
 from jax.sharding import PartitionSpec as P
 
 K = 4096
@@ -127,6 +130,376 @@
     return combined
 
 
+MESH = pl.DeviceIdType.MESH
+SINE = (6.28318516, -41.34165503, 81.60100405, -76.5497817, 39.53670129)
+
+
+def sine_of_turn(quarter):
+    square = quarter * quarter
+    total = SINE[-1] * square + SINE[-2]
+    for factor in SINE[-3::-1]:
+        total = total * square + factor
+    return total * quarter
+
+
+def cos_sin(turn):
+    turn = turn * (1.0 / 65536.0)
+    turn = turn - jnp.floor(turn + 0.5)
+    shifted_turn = turn - 0.25
+    shifted_turn = jnp.where(shifted_turn < -0.5, shifted_turn + 1.0, shifted_turn)
+    return (
+        sine_of_turn(0.25 - jnp.abs(turn)).astype(jnp.bfloat16),
+        sine_of_turn(0.25 - jnp.abs(shifted_turn)).astype(jnp.bfloat16),
+    )
+
+
+def columns_of(rows):
+    padded = jnp.concatenate([rows, jnp.zeros((5, rows.shape[1]), jnp.float32)], axis=0)
+    turned = padded.T
+    return [turned[:, axis : axis + 1] for axis in range(3)]
+
+
+def rows_of(rows):
+    return [rows[axis : axis + 1, :] for axis in range(3)]
+
+
+def turns(first, second):
+    return first[0] * second[0] + first[1] * second[1] + first[2] * second[2]
+
+
+def fused_kernel(
+    n,
+    groups,
+    feat_ref,
+    pos_ref,
+    nbr_ref,
+    wave_ref,
+    width_ref,
+    short_ref,
+    latw_ref,
+    mix_ref,
+    rate_ref,
+    outw_ref,
+    out_ref,
+    feat_buf,
+    pos_buf,
+    fused_w,
+    factors,
+    gathered,
+    phase_buf,
+    filt_buf,
+    message,
+    summed,
+    send_buf,
+    recv_buf,
+    own_sem,
+    feat_send,
+    feat_recv,
+    pos_send,
+    pos_recv,
+    fwd_send,
+    fwd_recv,
+    filt_send,
+    filt_recv,
+    msg_send,
+    msg_recv,
+):
+    me = lax.axis_index("atoms")
+    group = lax.axis_index("waves")
+    core = lax.rem(group, 2)
+    partner = group + 1 - 2 * core
+    half, channels = feat_ref.shape[1], feat_ref.shape[2]
+    rows = 2 * half
+    blocks_here = rows // BLOCK
+    local_kernels = short_ref.shape[0]
+    waves_each = wave_ref.shape[1] // n
+
+    def peer(step):
+        return lax.rem(me + step, n)
+
+    def source(step):
+        return lax.rem(me + n - step, n)
+
+    def feat_copy(step):
+        return pltpu.make_async_remote_copy(
+            src_ref=feat_ref.at[core],
+            dst_ref=feat_buf.at[me, core],
+            send_sem=feat_send.at[step],
+            recv_sem=feat_recv.at[step],
+            device_id={"atoms": peer(step)},
+            device_id_type=MESH,
+        )
+
+    def pos_copy(step):
+        return pltpu.make_async_remote_copy(
+            src_ref=pos_ref,
+            dst_ref=pos_buf.at[me],
+            send_sem=pos_send.at[step],
+            recv_sem=pos_recv.at[step],
+            device_id={"atoms": peer(step)},
+            device_id_type=MESH,
+        )
+
+    def forward_copy(step):
+        return pltpu.make_async_remote_copy(
+            src_ref=feat_buf.at[source(step), core],
+            dst_ref=feat_buf.at[source(step), core],
+            send_sem=fwd_send.at[step],
+            recv_sem=fwd_recv.at[step],
+            device_id={"waves": partner},
+            device_id_type=MESH,
+        )
+
+    def filt_copy(step):
+        return pltpu.make_async_remote_copy(
+            src_ref=filt_buf.at[me],
+            dst_ref=filt_buf.at[me],
+            send_sem=filt_send.at[step],
+            recv_sem=filt_recv.at[step],
+            device_id={"atoms": peer(step)},
+            device_id_type=MESH,
+        )
+
+    def msg_copy(step):
+        target = lax.rem(group + step, groups)
+        return pltpu.make_async_remote_copy(
+            src_ref=send_buf.at[target],
+            dst_ref=recv_buf.at[step],
+            send_sem=msg_send.at[step],
+            recv_sem=msg_recv.at[step],
+            device_id={"waves": target},
+            device_id_type=MESH,
+        )
+
+    own_feat = pltpu.make_async_copy(feat_ref, feat_buf.at[me], own_sem.at[0])
+    own_pos = pltpu.make_async_copy(pos_ref, pos_buf.at[me], own_sem.at[1])
+    own_feat.start()
+    own_pos.start()
+
+    barrier = pltpu.get_barrier_semaphore()
+    for step in range(1, n):
+        pl.semaphore_signal(barrier, inc=1, device_id={"atoms": peer(step)}, device_id_type=MESH)
+    for step in range(1, groups):
+        pl.semaphore_signal(
+            barrier,
+            inc=1,
+            device_id={"waves": lax.rem(group + step, groups)},
+            device_id_type=MESH,
+        )
+    pl.semaphore_wait(barrier, n - 1 + groups - 1)
+
+    for step in range(1, n):
+        pos_copy(step).start()
+        feat_copy(step).start()
+
+    fused_w[...] = jnp.dot(
+        latw_ref[...].astype(jnp.float32),
+        mix_ref[...],
+        precision=lax.Precision.HIGHEST,
+        preferred_element_type=jnp.float32,
+    ).astype(jnp.bfloat16)
+    spots = columns_of(pos_ref[...].astype(jnp.float32))
+
+    def phase_step(which, carry):
+        begin = pl.multiple_of(which * waves_each, waves_each)
+        waves = rows_of(wave_ref[:, pl.ds(begin, waves_each)].astype(jnp.float32))
+        cosine, sine = cos_sin(turns(spots, waves))
+        phase_buf[which] = jnp.concatenate([cosine, sine], axis=1)
+        return carry
+
+    lax.fori_loop(0, n, phase_step, 0)
+
+    begin = pl.multiple_of(me * waves_each, waves_each)
+    own_waves = columns_of(wave_ref[:, pl.ds(begin, waves_each)].astype(jnp.float32))
+    factors[...] = jnp.zeros_like(factors)
+    gathered[...] = jnp.zeros_like(gathered)
+    own_feat.wait()
+    own_pos.wait()
+    norm_scale = 1.0 / math.sqrt(NBR * BLOCK)
+
+    def shard_step(step, carry):
+        @pl.when(step < n)
+        def _():
+            feat_copy(step).wait_recv()
+            forward_copy(step).start()
+
+        now = step - 1
+
+        @pl.when(now > 0)
+        def _():
+            pos_copy(now).wait_recv()
+            forward_copy(now).wait_recv()
+
+        origin = source(now)
+        feats = feat_buf[origin].reshape(rows, channels)
+        near = rows_of(pos_buf[origin].astype(jnp.float32))
+        latent = jnp.dot(feats, fused_w[...], preferred_element_type=jnp.float32)
+        cosine, sine = cos_sin(turns(own_waves, near))
+        phases = jnp.concatenate([cosine, sine], axis=0)
+        factors[...] += jnp.dot(
+            phases, latent.astype(jnp.bfloat16), preferred_element_type=jnp.float32
+        )
+        lane_block = lax.broadcasted_iota(jnp.int32, (1, rows), 1) // BLOCK
+        for block in range(blocks_here):
+            keep = jnp.zeros((1, rows), jnp.float32)
+            for near_block in range(blocks_here):
+                number = origin * blocks_here + near_block
+                listed = jnp.float32(0.0)
+                for slot in range(NBR):
+                    listed += jnp.where(nbr_ref[block, slot] == number, norm_scale, 0.0)
+                keep = keep + jnp.where(lane_block == near_block, listed, 0.0)
+            low = block * BLOCK
+            dist_sq = None
+            for axis in range(3):
+                gap = jnp.abs(spots[axis][low : low + BLOCK] - near[axis]) * (1.0 / 65536.0)
+                gap = jnp.minimum(gap, 1.0 - gap)
+                dist_sq = gap * gap if dist_sq is None else dist_sq + gap * gap
+            distance = jnp.sqrt(dist_sq)
+            smooth = jnp.maximum(1.0 - dist_sq * (1.0 / (cutoff * cutoff)), 0.0)
+            smooth = smooth * smooth * keep
+            for kernel in range(local_kernels):
+                center = (group * local_kernels + kernel).astype(jnp.float32) * (
+                    cutoff / (RADIAL - 1)
+                )
+                shaped = (distance - center) / width_ref[kernel]
+                weights = (jnp.exp(-(shaped * shaped)) * smooth).astype(jnp.bfloat16)
+                gathered[kernel, low : low + BLOCK, :] += jnp.dot(
+                    weights, feats, preferred_element_type=jnp.float32
+                )
+        return carry
+
+    lax.fori_loop(1, n + 1, shard_step, 0)
+
+    lengths = turns(own_waves, own_waves)
+    gain = jnp.exp(-lengths * rate_ref[...]) * (1.0 / math.sqrt(rows * n))
+    filt_buf[me] = (factors[...] * jnp.concatenate([gain, gain], axis=0)).astype(jnp.bfloat16)
+    for step in range(1, n):
+        filt_copy(step).start()
+
+    short = jnp.zeros(message.shape, jnp.float32)
+    for kernel in range(local_kernels):
+        short += jnp.dot(
+            gathered[kernel].astype(jnp.bfloat16),
+            short_ref[kernel],
+            preferred_element_type=jnp.float32,
+        )
+    message[...] = short
+    summed[...] = jnp.dot(phase_buf[me], filt_buf[me], preferred_element_type=jnp.float32)
+
+    def long_step(step, carry):
+        filt_copy(step).wait_recv()
+        origin = source(step)
+        summed[...] += jnp.dot(
+            phase_buf[origin], filt_buf[origin], preferred_element_type=jnp.float32
+        )
+        return carry
+
+    lax.fori_loop(1, n, long_step, 0)
+
+    reduced = (summed[...] * (1.0 / math.sqrt(K))).astype(jnp.bfloat16)
+    width = out_ref.shape[1]
+    for target in range(groups):
+        low = target * width
+        part = message[:, low : low + width] + jnp.dot(
+            reduced, outw_ref[:, low : low + width], preferred_element_type=jnp.float32
+        )
+        send_buf[target] = part.astype(jnp.bfloat16)
+    for step in range(1, groups):
+        msg_copy(step).start()
+    total = send_buf[group].astype(jnp.float32)
+    for step in range(1, groups):
+        msg_copy(step).wait_recv()
+        total += recv_buf[step].astype(jnp.float32)
+    out_ref[...] = total.astype(out_ref.dtype)
+    for step in range(1, n):
+        feat_copy(step).wait_send()
+        pos_copy(step).wait_send()
+        forward_copy(step).wait_send()
+        filt_copy(step).wait_send()
+    for step in range(1, groups):
+        msg_copy(step).wait_send()
+
+
+def fused(
+    features,
+    positions,
+    neighbours,
+    wavevectors,
+    radial_width,
+    short_weight,
+    latent_weight,
+    mix_weight,
+    filter_rate,
+    out_weight,
+):
+    n = lax.axis_size("atoms")
+    groups = lax.axis_size("waves")
+    rows, channels = features.shape
+    latents = latent_weight.shape[1]
+    waves_each = wavevectors.shape[1] // n
+    local_kernels = radial_width.shape[0]
+    vmem = pl.BlockSpec(memory_space=pltpu.VMEM)
+    smem = pl.BlockSpec(memory_space=pltpu.SMEM)
+    dma = pltpu.SemaphoreType.DMA
+    return pl.pallas_call(
+        functools.partial(fused_kernel, n, groups),
+        out_shape=jax.ShapeDtypeStruct((rows, channels // groups), jnp.bfloat16),
+        in_specs=[vmem, vmem, smem, vmem, smem, vmem, vmem, vmem, vmem, vmem],
+        out_specs=vmem,
+        scratch_shapes=[
+            pltpu.VMEM((n, 2, rows // 2, channels), jnp.bfloat16),
+            pltpu.VMEM((n, 3, rows), jnp.int32),
+            pltpu.VMEM((channels, latents), jnp.bfloat16),
+            pltpu.VMEM((2 * waves_each, latents), jnp.float32),
+            pltpu.VMEM((local_kernels, rows, channels), jnp.float32),
+            pltpu.VMEM((n, rows, 2 * waves_each), jnp.bfloat16),
+            pltpu.VMEM((n, 2 * waves_each, latents), jnp.bfloat16),
+            pltpu.VMEM((rows, channels), jnp.float32),
+            pltpu.VMEM((rows, latents), jnp.float32),
+            pltpu.VMEM((groups, rows, channels // groups), jnp.bfloat16),
+            pltpu.VMEM((groups, rows, channels // groups), jnp.bfloat16),
+            dma((2,)),
+            dma((n,)),
+            dma((n,)),
+            dma((n,)),
+            dma((n,)),
+            dma((n,)),
+            dma((n,)),
+            dma((n,)),
+            dma((n,)),
+            dma((groups,)),
+            dma((groups,)),
+        ],
+        compiler_params=pltpu.CompilerParams(
+            collective_id=0, has_side_effects=True, vmem_limit_bytes=48 * 1024 * 1024
+        ),
+    )(
+        features.reshape(2, rows // 2, channels),
+        positions,
+        neighbours,
+        wavevectors,
+        radial_width,
+        short_weight,
+        latent_weight,
+        mix_weight,
+        filter_rate.reshape(1, latents),
+        out_weight,
+    )
+
+
+def layer(*arrays):
+    features, wavevectors = arrays[0], arrays[3]
+    n = lax.axis_size("atoms")
+    groups = lax.axis_size("waves")
+    rows = features.shape[0]
+    reach_hops = -(-REACH // (rows // BLOCK))
+    covers_all = 2 * reach_hops + 1 >= n
+    if covers_all and groups % 2 == 0 and rows % (2 * BLOCK) == 0:
+        if wavevectors.shape[1] % (128 * n) == 0:
+            return fused(*arrays)
+    return local(*arrays)
+
+
 def solution(mesh):
     placed = (
         P("atoms", None),
@@ -141,5 +514,5 @@
         P(),
     )
     return jax.shard_map(
-        local, mesh=mesh, in_specs=placed, out_specs=P("atoms", "waves"), check_vma=False
-    )
+        layer, mesh=mesh, in_specs=placed, out_specs=P("atoms", "waves"), check_vma=False
+    )

time: 188 us -> 69.5 us (0.37)
  the two profiles are of different devices: /device:TPU:1 before, /device:TPU:13 now
where the time goes in v1:
time: 69.5 us; the launch traced here: 69.1 us
  Pallas kernels  61.4 us (88%)
  local copies, waits for them, and re-layouts  7.75 us (11%)
    pallas_call x1, Pallas kernels, fused(): pl.pallas_call(functools.partial(fused_kernel, n, groups), out_shape=jax....  61.4 us
    unnamed x21, local copies, waits for them, and re-layouts  7.75 us

profile of v1, /device:TPU:13, one launch (start us, length us, event | category | flops | bytes accessed | tf_op | source)
XLA Modules:
  0.0 69.1 jit_solution(13972302567495008988)
XLA Ops:
  0.0 0.0 copy-start.8
  0.0 0.0 copy-start.7
  0.0 0.0 copy-start.9
  0.0 0.7 copy-done.8
  0.7 0.0 copy-done.7
  0.7 0.0 copy-done.9
  0.7 0.0 copy-start
  0.7 1.2 %copy-done = bf16[2,512,512]{2,1,0:T(8,128)(2,1)S(1)} copy-done((bf16[2,512,512]{2,1,0:T(8,128)(2,1)S(1)}, bf16[2,512,512]{2,1,0:T(8,128)(2,1)}, u32[]{:S(2)}) %copy-start) | copy-done | bytes 1048600
  1.9 0.0 copy-start.1
  1.9 0.9 %copy-done.1 = bf16[256,512]{1,0:T(8,128)(2,1)S(1)} copy-done((bf16[256,512]{1,0:T(8,128)(2,1)S(1)}, bf16[256,512]{1,0:T(8,128)(2,1)}, u32[]{:S(2)}) %copy-start.1) | copy-done | bytes 262168
  2.9 0.0 copy-start.2
  2.9 0.9 %copy-done.2 = bf16[512,256]{1,0:T(8,128)(2,1)S(1)} copy-done((bf16[512,256]{1,0:T(8,128)(2,1)S(1)}, bf16[512,256]{1,0:T(8,128)(2,1)}, u32[]{:S(2)}) %copy-start.2) | copy-done | bytes 262168
  3.8 0.0 copy-start.3
  3.8 0.9 %copy-done.3 = f32[256,256]{1,0:T(8,128)S(1)} copy-done((f32[256,256]{1,0:T(8,128)S(1)}, f32[256,256]{1,0:T(8,128)}, u32[]{:S(2)}) %copy-start.3) | copy-done | bytes 262168
  4.8 0.0 copy-start.4
  4.8 0.9 %copy-done.4 = bf16[256,512]{1,0:T(8,128)(2,1)S(1)} copy-done((bf16[256,512]{1,0:T(8,128)(2,1)S(1)}, bf16[256,512]{1,0:T(8,128)(2,1)}, u32[]{:S(2)}) %copy-start.4) | copy-done | bytes 262168
  5.7 0.0 copy-start.5
  5.7 0.7 %copy-done.5 = s32[3,1024]{1,0:T(4,128)S(1)} copy-done((s32[3,1024]{1,0:T(4,128)S(1)}, s32[3,1024]{1,0:T(4,128)}, u32[]{:S(2)}) %copy-start.5) | copy-done | bytes 12312
  6.4 0.0 copy-start.6
  6.4 0.7 copy-done.6
  7.1 61.4 %shard_map.100 = bf16[256,128]{1,0:T(8,128)(2,1)S(1)} custom-call(bf16[2,128,512]{2,1,0:T(8,128)(2,1)S(1)} %bitcast.2, s32[3,256]{1,0:T(4,128)S(1)} %copy-done.6, s32[2,12]{1,0:T(2,128)S(1)} %copy-done.7, s32[3,1024]{1,0:T(4,128)S(1)} %copy-done.5, f32[2]{0:T(128)S(1)} %copy-done.9, bf16[2,512,512]{2,1,0:T(8,128)(2,1)S(1)} %copy-done, ...), custom_call_target="tpu_custom_call" | custom-call | tf_op jit(solution)/shard_map/pallas_call | solution.py:444
  68.5 0.6 copy.12
Async XLA Ops:
  0.0 0.7 copy-start.8
  0.0 0.7 %copy-start.7 = (s32[2,12]{1,0:T(2,128)S(1)}, s32[2,12]{1,0:T(2,128)}, u32[]{:S(2)}) copy-start(s32[2,12]{1,0:T(2,128)} %nbr_ref.1) | copy-start | bytes 292
  0.0 0.7 %copy-start.9 = (f32[2]{0:T(128)S(1)}, f32[2]{0:T(128)}, u32[]{:S(2)}) copy-start(f32[2]{0:T(128)} %width_ref.1) | copy-start | bytes 28
  0.7 1.2 %copy-start = (bf16[2,512,512]{2,1,0:T(8,128)(2,1)S(1)}, bf16[2,512,512]{2,1,0:T(8,128)(2,1)}, u32[]{:S(2)}) copy-start(bf16[2,512,512]{2,1,0:T(8,128)(2,1)} %short_ref.1) | copy-start | bytes 3145732
  1.9 0.9 %copy-start.1 = (bf16[256,512]{1,0:T(8,128)(2,1)S(1)}, bf16[256,512]{1,0:T(8,128)(2,1)}, u32[]{:S(2)}) copy-start(bf16[256,512]{1,0:T(8,128)(2,1)} %param.10) | copy-start | bytes 786436
  2.9 0.9 %copy-start.2 = (bf16[512,256]{1,0:T(8,128)(2,1)S(1)}, bf16[512,256]{1,0:T(8,128)(2,1)}, u32[]{:S(2)}) copy-start(bf16[512,256]{1,0:T(8,128)(2,1)} %latw_ref.1) | copy-start | bytes 786436
  3.8 0.9 %copy-start.3 = (f32[256,256]{1,0:T(8,128)S(1)}, f32[256,256]{1,0:T(8,128)}, u32[]{:S(2)}) copy-start(f32[256,256]{1,0:T(8,128)} %mix_ref.1) | copy-start | bytes 786436
  4.8 0.9 %copy-start.4 = (bf16[256,512]{1,0:T(8,128)(2,1)S(1)}, bf16[256,512]{1,0:T(8,128)(2,1)}, u32[]{:S(2)}) copy-start(bf16[256,512]{1,0:T(8,128)(2,1)} %outw_ref.1) | copy-start | bytes 786436
  5.7 0.7 %copy-start.5 = (s32[3,1024]{1,0:T(4,128)S(1)}, s32[3,1024]{1,0:T(4,128)}, u32[]{:S(2)}) copy-start(s32[3,1024]{1,0:T(4,128)} %wave_ref.1) | copy-start | bytes 36868
  6.4 0.7 copy-start.6

commit v2 on v1

--- a/solution.py
+++ b/solution.py
@@ -173,14 +173,20 @@
     feat_ref,
     pos_ref,
     nbr_ref,
+    wave_in,
+    width_ref,
+    short_in,
+    latw_in,
+    mix_in,
+    rate_in,
+    outw_in,
+    out_ref,
     wave_ref,
-    width_ref,
     short_ref,
     latw_ref,
     mix_ref,
     rate_ref,
     outw_ref,
-    out_ref,
     feat_buf,
     pos_buf,
     fused_w,
@@ -193,17 +199,25 @@
     send_buf,
     recv_buf,
     own_sem,
-    feat_send,
-    feat_recv,
+    feat_up,
+    feat_down,
+    feat_line,
+    feat_side_send,
+    feat_side,
     pos_send,
     pos_recv,
     fwd_send,
     fwd_recv,
-    filt_send,
-    filt_recv,
+    filt_up,
+    filt_down,
+    filt_line,
+    filt_side_send,
+    filt_side,
     msg_send,
     msg_recv,
 ):
+    feat_sends = (feat_up, feat_down, feat_line, feat_side_send, feat_side)
+    filt_sends = (filt_up, filt_down, filt_line, filt_side_send, filt_side)
     me = lax.axis_index("atoms")
     group = lax.axis_index("waves")
     core = lax.rem(group, 2)
@@ -214,21 +228,92 @@
     local_kernels = short_ref.shape[0]
     waves_each = wave_ref.shape[1] // n
 
+    lines = n // 2
+    line, side = me // 2, lax.rem(me, 2)
+
     def peer(step):
         return lax.rem(me + step, n)
 
     def source(step):
         return lax.rem(me + n - step, n)
 
-    def feat_copy(step):
+    def ranked(rank):
+        closest = jnp.minimum(line, lines - 1 - line)
+        away = (rank + 1) // 2
+        near_line = jnp.where(lax.rem(rank, 2) == 1, line - away, line + away)
+        far_line = jnp.where(line < lines - 1 - line, rank, lines - 1 - rank)
+        return jnp.where(rank <= 2 * closest, near_line, far_line)
+
+    def line_copy(sends, piece, shard_line, direction):
+        up_send, down_send, line_recv, _, _ = sends
         return pltpu.make_async_remote_copy(
-            src_ref=feat_ref.at[core],
-            dst_ref=feat_buf.at[me, core],
-            send_sem=feat_send.at[step],
-            recv_sem=feat_recv.at[step],
-            device_id={"atoms": peer(step)},
+            src_ref=piece[0],
+            dst_ref=piece[1],
+            send_sem=(up_send if direction > 0 else down_send).at[shard_line],
+            recv_sem=line_recv.at[shard_line],
+            device_id={"atoms": me + 2 * direction},
             device_id_type=MESH,
         )
+
+    def side_copy(sends, piece, shard_line):
+        return pltpu.make_async_remote_copy(
+            src_ref=piece[0],
+            dst_ref=piece[1],
+            send_sem=sends[3].at[shard_line],
+            recv_sem=sends[4].at[shard_line],
+            device_id={"atoms": me + 1 - 2 * side},
+            device_id_type=MESH,
+        )
+
+    def feat_piece(shard_line, shard_side):
+        place = feat_buf.at[2 * shard_line + shard_side, core]
+        return place, place
+
+    def filt_piece(shard_line, shard_side):
+        place = filt_buf.at[2 * shard_line + shard_side]
+        return place, place
+
+    def send_own(sends, piece):
+        @pl.when(line < lines - 1)
+        def _():
+            line_copy(sends, piece, line, 1).start()
+
+        @pl.when(line > 0)
+        def _():
+            line_copy(sends, piece, line, -1).start()
+
+        side_copy(sends, piece, line).start()
+
+    def pass_on(sends, piece_of, shard_line):
+        piece = piece_of(shard_line, side)
+        line_copy(sends, piece, shard_line, 1).wait_recv()
+
+        @pl.when((shard_line < line) & (line < lines - 1))
+        def _():
+            line_copy(sends, piece, shard_line, 1).start()
+
+        @pl.when((shard_line > line) & (line > 0))
+        def _():
+            line_copy(sends, piece, shard_line, -1).start()
+
+        side_copy(sends, piece, shard_line).start()
+
+    def finish(sends, piece_of):
+        def one(shard_line, carry):
+            piece = piece_of(shard_line, side)
+
+            @pl.when((shard_line <= line) & (line < lines - 1))
+            def _():
+                line_copy(sends, piece, shard_line, 1).wait_send()
+
+            @pl.when((shard_line >= line) & (line > 0))
+            def _():
+                line_copy(sends, piece, shard_line, -1).wait_send()
+
+            side_copy(sends, piece, shard_line).wait_send()
+            return carry
+
+        lax.fori_loop(0, lines, one, 0)
 
     def pos_copy(step):
         return pltpu.make_async_remote_copy(
@@ -240,23 +325,13 @@
             device_id_type=MESH,
         )
 
-    def forward_copy(step):
+    def forward_copy(origin):
         return pltpu.make_async_remote_copy(
-            src_ref=feat_buf.at[source(step), core],
-            dst_ref=feat_buf.at[source(step), core],
-            send_sem=fwd_send.at[step],
-            recv_sem=fwd_recv.at[step],
+            src_ref=feat_buf.at[origin, core],
+            dst_ref=feat_buf.at[origin, core],
+            send_sem=fwd_send.at[origin],
+            recv_sem=fwd_recv.at[origin],
             device_id={"waves": partner},
-            device_id_type=MESH,
-        )
-
-    def filt_copy(step):
-        return pltpu.make_async_remote_copy(
-            src_ref=filt_buf.at[me],
-            dst_ref=filt_buf.at[me],
-            send_sem=filt_send.at[step],
-            recv_sem=filt_recv.at[step],
-            device_id={"atoms": peer(step)},
             device_id_type=MESH,
         )
 
@@ -273,8 +348,25 @@
 
     own_feat = pltpu.make_async_copy(feat_ref, feat_buf.at[me], own_sem.at[0])
     own_pos = pltpu.make_async_copy(pos_ref, pos_buf.at[me], own_sem.at[1])
+    loads = [
+        pltpu.make_async_copy(held, kept, own_sem.at[2 + which])
+        for which, (held, kept) in enumerate(
+            (
+                (wave_in, wave_ref),
+                (mix_in, mix_ref),
+                (latw_in, latw_ref),
+                (rate_in, rate_ref),
+                (short_in, short_ref),
+                (outw_in, outw_ref),
+            )
+        )
+    ]
+    own_pos.start()
+    for load in loads[:4]:
+        load.start()
     own_feat.start()
-    own_pos.start()
+    for load in loads[4:]:
+        load.start()
 
     barrier = pltpu.get_barrier_semaphore()
     for step in range(1, n):
@@ -288,49 +380,36 @@
         )
     pl.semaphore_wait(barrier, n - 1 + groups - 1)
 
+    send_own(feat_sends, (feat_ref.at[core], feat_buf.at[me, core]))
     for step in range(1, n):
         pos_copy(step).start()
-        feat_copy(step).start()
-
+
+    own_pos.wait()
+    for load in loads[:4]:
+        load.wait()
     fused_w[...] = jnp.dot(
         latw_ref[...].astype(jnp.float32),
         mix_ref[...],
         precision=lax.Precision.HIGHEST,
         preferred_element_type=jnp.float32,
     ).astype(jnp.bfloat16)
-    spots = columns_of(pos_ref[...].astype(jnp.float32))
-
-    def phase_step(which, carry):
+    spots = columns_of(pos_buf[me].astype(jnp.float32))
+
+    def phase_step(which):
         begin = pl.multiple_of(which * waves_each, waves_each)
         waves = rows_of(wave_ref[:, pl.ds(begin, waves_each)].astype(jnp.float32))
         cosine, sine = cos_sin(turns(spots, waves))
         phase_buf[which] = jnp.concatenate([cosine, sine], axis=1)
-        return carry
-
-    lax.fori_loop(0, n, phase_step, 0)
 
     begin = pl.multiple_of(me * waves_each, waves_each)
     own_waves = columns_of(wave_ref[:, pl.ds(begin, waves_each)].astype(jnp.float32))
     factors[...] = jnp.zeros_like(factors)
     gathered[...] = jnp.zeros_like(gathered)
     own_feat.wait()
-    own_pos.wait()
     norm_scale = 1.0 / math.sqrt(NBR * BLOCK)
 
-    def shard_step(step, carry):
-        @pl.when(step < n)
-        def _():
-            feat_copy(step).wait_recv()
-            forward_copy(step).start()
-
-        now = step - 1
-
-        @pl.when(now > 0)
-        def _():
-            pos_copy(now).wait_recv()
-            forward_copy(now).wait_recv()
-
-        origin = source(now)
+    def use_shard(origin):
+        phase_step(origin)
         feats = feat_buf[origin].reshape(rows, channels)
         near = rows_of(pos_buf[origin].astype(jnp.float32))
         latent = jnp.dot(feats, fused_w[...], preferred_element_type=jnp.float32)
@@ -361,21 +440,47 @@
                 center = (group * local_kernels + kernel).astype(jnp.float32) * (
                     cutoff / (RADIAL - 1)
                 )
-                shaped = (distance - center) / width_ref[kernel]
+                shaped = (distance - center) * (1.0 / width_ref[kernel])
                 weights = (jnp.exp(-(shaped * shaped)) * smooth).astype(jnp.bfloat16)
                 gathered[kernel, low : low + BLOCK, :] += jnp.dot(
                     weights, feats, preferred_element_type=jnp.float32
                 )
+
+    def gather_step(rank, carry):
+        @pl.when(rank < lines)
+        def _():
+            shard_line = ranked(rank)
+            pass_on(feat_sends, feat_piece, shard_line)
+            forward_copy(2 * shard_line + side).start()
+
+        shard_line = ranked(rank - 1)
+        other = 2 * shard_line + 1 - side
+        side_copy(feat_sends, feat_piece(shard_line, 1 - side), shard_line).wait_recv()
+        forward_copy(other).start()
+
+        def use_step(which, carry):
+            origin = 2 * shard_line + jnp.where(which == 0, side, 1 - side)
+
+            @pl.when(origin != me)
+            def _():
+                pos_copy(lax.rem(me - origin + n, n)).wait_recv()
+                forward_copy(origin).wait_recv()
+
+            use_shard(origin)
+            return carry
+
+        lax.fori_loop(0, 2, use_step, 0)
         return carry
 
-    lax.fori_loop(1, n + 1, shard_step, 0)
+    lax.fori_loop(1, lines + 1, gather_step, 0)
 
     lengths = turns(own_waves, own_waves)
     gain = jnp.exp(-lengths * rate_ref[...]) * (1.0 / math.sqrt(rows * n))
     filt_buf[me] = (factors[...] * jnp.concatenate([gain, gain], axis=0)).astype(jnp.bfloat16)
-    for step in range(1, n):
-        filt_copy(step).start()
-
+    send_own(filt_sends, filt_piece(line, side))
+
+    for load in loads[4:]:
+        load.wait()
     short = jnp.zeros(message.shape, jnp.float32)
     for kernel in range(local_kernels):
         short += jnp.dot(
@@ -386,15 +491,28 @@
     message[...] = short
     summed[...] = jnp.dot(phase_buf[me], filt_buf[me], preferred_element_type=jnp.float32)
 
-    def long_step(step, carry):
-        filt_copy(step).wait_recv()
-        origin = source(step)
+    def long_step(rank, carry):
+        @pl.when(rank < lines)
+        def _():
+            pass_on(filt_sends, filt_piece, ranked(rank))
+
+        shard_line = ranked(rank - 1)
+        side_copy(filt_sends, filt_piece(shard_line, 1 - side), shard_line).wait_recv()
+        other = 2 * shard_line + 1 - side
         summed[...] += jnp.dot(
-            phase_buf[origin], filt_buf[origin], preferred_element_type=jnp.float32
-        )
+            phase_buf[other], filt_buf[other], preferred_element_type=jnp.float32
+        )
+
+        @pl.when(rank < lines)
+        def _():
+            origin = 2 * ranked(rank) + side
+            summed[...] += jnp.dot(
+                phase_buf[origin], filt_buf[origin], preferred_element_type=jnp.float32
+            )
+
         return carry
 
-    lax.fori_loop(1, n, long_step, 0)
+    lax.fori_loop(1, lines + 1, long_step, 0)
 
     reduced = (summed[...] * (1.0 / math.sqrt(K))).astype(jnp.bfloat16)
     width = out_ref.shape[1]
@@ -411,11 +529,15 @@
         msg_copy(step).wait_recv()
         total += recv_buf[step].astype(jnp.float32)
     out_ref[...] = total.astype(out_ref.dtype)
-    for step in range(1, n):
-        feat_copy(step).wait_send()
+    finish(feat_sends, feat_piece)
+    finish(filt_sends, filt_piece)
+
+    def finish_step(step, carry):
         pos_copy(step).wait_send()
-        forward_copy(step).wait_send()
-        filt_copy(step).wait_send()
+        forward_copy(peer(step)).wait_send()
+        return carry
+
+    lax.fori_loop(1, n, finish_step, 0)
     for step in range(1, groups):
         msg_copy(step).wait_send()
 
@@ -439,14 +561,21 @@
     waves_each = wavevectors.shape[1] // n
     local_kernels = radial_width.shape[0]
     vmem = pl.BlockSpec(memory_space=pltpu.VMEM)
+    held = pl.BlockSpec(memory_space=pl.ANY)
     smem = pl.BlockSpec(memory_space=pltpu.SMEM)
     dma = pltpu.SemaphoreType.DMA
     return pl.pallas_call(
         functools.partial(fused_kernel, n, groups),
         out_shape=jax.ShapeDtypeStruct((rows, channels // groups), jnp.bfloat16),
-        in_specs=[vmem, vmem, smem, vmem, smem, vmem, vmem, vmem, vmem, vmem],
+        in_specs=[held, held, smem, held, smem, held, held, held, held, held],
         out_specs=vmem,
         scratch_shapes=[
+            pltpu.VMEM(wavevectors.shape, jnp.int32),
+            pltpu.VMEM(short_weight.shape, jnp.bfloat16),
+            pltpu.VMEM(latent_weight.shape, jnp.bfloat16),
+            pltpu.VMEM(mix_weight.shape, jnp.float32),
+            pltpu.VMEM((1, latents), jnp.float32),
+            pltpu.VMEM(out_weight.shape, jnp.bfloat16),
             pltpu.VMEM((n, 2, rows // 2, channels), jnp.bfloat16),
             pltpu.VMEM((n, 3, rows), jnp.int32),
             pltpu.VMEM((channels, latents), jnp.bfloat16),
@@ -458,20 +587,14 @@
             pltpu.VMEM((rows, latents), jnp.float32),
             pltpu.VMEM((groups, rows, channels // groups), jnp.bfloat16),
             pltpu.VMEM((groups, rows, channels // groups), jnp.bfloat16),
-            dma((2,)),
-            dma((n,)),
-            dma((n,)),
-            dma((n,)),
-            dma((n,)),
-            dma((n,)),
-            dma((n,)),
-            dma((n,)),
-            dma((n,)),
-            dma((groups,)),
-            dma((groups,)),
+            dma((8,)),
+            *[dma((n // 2,)) for _ in range(5)],
+            *[dma((n,)) for _ in range(4)],
+            *[dma((n // 2,)) for _ in range(5)],
+            *[dma((groups,)) for _ in range(2)],
         ],
         compiler_params=pltpu.CompilerParams(
-            collective_id=0, has_side_effects=True, vmem_limit_bytes=48 * 1024 * 1024
+            collective_id=0, has_side_effects=True, vmem_limit_bytes=67043328
         ),
     )(
         features.reshape(2, rows // 2, channels),
@@ -494,7 +617,7 @@
     rows = features.shape[0]
     reach_hops = -(-REACH // (rows // BLOCK))
     covers_all = 2 * reach_hops + 1 >= n
-    if covers_all and groups % 2 == 0 and rows % (2 * BLOCK) == 0:
+    if covers_all and groups % 2 == 0 and n % 2 == 0 and rows % (2 * BLOCK) == 0:
         if wavevectors.shape[1] % (128 * n) == 0:
             return fused(*arrays)
     return local(*arrays)

time: 69.5 us -> 55 us (0.79)
  the two profiles are of different devices: /device:TPU:13 before, /device:TPU:1 now
where the time goes in v2:
time: 55 us; the launch traced here: 54.9 us
  Pallas kernels  53.4 us (97%)
  local copies, waits for them, and re-layouts  1.47 us (3%)
    pallas_call x1, Pallas kernels, fused(): pl.pallas_call(functools.partial(fused_kernel, n, groups), out_shape=jax....  53.4 us
    unnamed x1, local copies, waits for them, and re-layouts  1.47 us

profile of v2, /device:TPU:1, one launch (start us, length us, event | category | flops | bytes accessed | tf_op | source)
XLA Modules:
  0.0 54.9 jit_solution(2381547791659823632)
XLA Ops:
  0.0 53.4 %shard_map.100 = bf16[256,128]{1,0:T(8,128)(2,1)} custom-call(bf16[2,128,512]{2,1,0:T(8,128)(2,1)} %bitcast.2, s32[3,256]{1,0:T(4,128)} %pos_ref.1, s32[2,12]{1,0:T(2,128)} %nbr_ref.1, s32[3,1024]{1,0:T(4,128)} %wave_in.1, f32[2]{0:T(128)} %width_ref.1, bf16[2,512,512]{2,1,0:T(8,128)(2,1)} %short_in.1, bf16[512,256]{1,0:T(8,128)(2,1)} %latw_in.1, ...), custom_call_target="tpu_custom_call" | custom-call | tf_op jit(solution)/shard_map/pallas_call | solution.py:567
  53.4 1.5 %copy.12 = bf16[256,128]{1,0:T(8,128)(2,1)} copy(bf16[256,128]{1,0:T(8,128)(2,1)} %shard_map.100) | data formatting | bytes 131072

commit v3 on v2

--- a/solution.py
+++ b/solution.py
@@ -193,7 +193,11 @@
     factors,
     gathered,
     phase_buf,
+    wave_cols,
+    filt_cols,
     filt_buf,
+    sum_send_buf,
+    sum_buf,
     message,
     summed,
     send_buf,
@@ -208,16 +212,12 @@
     pos_recv,
     fwd_send,
     fwd_recv,
-    filt_up,
-    filt_down,
-    filt_line,
-    filt_side_send,
-    filt_side,
+    sum_send,
+    sum_recv,
     msg_send,
     msg_recv,
 ):
     feat_sends = (feat_up, feat_down, feat_line, feat_side_send, feat_side)
-    filt_sends = (filt_up, filt_down, filt_line, filt_side_send, filt_side)
     me = lax.axis_index("atoms")
     group = lax.axis_index("waves")
     core = lax.rem(group, 2)
@@ -226,7 +226,9 @@
     rows = 2 * half
     blocks_here = rows // BLOCK
     local_kernels = short_ref.shape[0]
-    waves_each = wave_ref.shape[1] // n
+    waves_each = wave_ref.shape[1] // 2
+    part = mix_ref.shape[1] // (n // 2)
+    per_tile = 128 // part
 
     lines = n // 2
     line, side = me // 2, lax.rem(me, 2)
@@ -269,10 +271,6 @@
         place = feat_buf.at[2 * shard_line + shard_side, core]
         return place, place
 
-    def filt_piece(shard_line, shard_side):
-        place = filt_buf.at[2 * shard_line + shard_side]
-        return place, place
-
     def send_own(sends, piece):
         @pl.when(line < lines - 1)
         def _():
@@ -332,6 +330,16 @@
             send_sem=fwd_send.at[origin],
             recv_sem=fwd_recv.at[origin],
             device_id={"waves": partner},
+            device_id_type=MESH,
+        )
+
+    def sum_copy(step):
+        return pltpu.make_async_remote_copy(
+            src_ref=sum_send_buf.at[peer(step)],
+            dst_ref=sum_buf.at[me],
+            send_sem=sum_send.at[step],
+            recv_sem=sum_recv.at[step],
+            device_id={"atoms": peer(step)},
             device_id_type=MESH,
         )
 
@@ -387,36 +395,47 @@
     own_pos.wait()
     for load in loads[:4]:
         load.wait()
+    tile = pl.ds(pl.multiple_of((line // per_tile) * 128, 128), 128)
     fused_w[...] = jnp.dot(
         latw_ref[...].astype(jnp.float32),
-        mix_ref[...],
+        mix_ref[:, tile],
         precision=lax.Precision.HIGHEST,
         preferred_element_type=jnp.float32,
     ).astype(jnp.bfloat16)
     spots = columns_of(pos_buf[me].astype(jnp.float32))
 
-    def phase_step(which):
-        begin = pl.multiple_of(which * waves_each, waves_each)
-        waves = rows_of(wave_ref[:, pl.ds(begin, waves_each)].astype(jnp.float32))
-        cosine, sine = cos_sin(turns(spots, waves))
-        phase_buf[which] = jnp.concatenate([cosine, sine], axis=1)
-
-    begin = pl.multiple_of(me * waves_each, waves_each)
+    begin = pl.multiple_of(side * waves_each, waves_each)
     own_waves = columns_of(wave_ref[:, pl.ds(begin, waves_each)].astype(jnp.float32))
+    for axis in range(3):
+        wave_cols[axis] = jnp.broadcast_to(own_waves[axis], (waves_each, 128))
+    chunk = 64
+
+    def phase_rows(origin, near):
+        def some(which, carry):
+            low = pl.multiple_of(which * chunk, chunk)
+            waves = [wave_cols[axis, pl.ds(low, chunk), :] for axis in range(3)]
+            for start in range(0, rows, 128):
+                spot = [row[:, start : start + 128] for row in near]
+                cosine, sine = cos_sin(turns(waves, spot))
+                phase_buf[origin, pl.ds(low, chunk), start : start + 128] = cosine
+                high = pl.multiple_of(waves_each + low, chunk)
+                phase_buf[origin, pl.ds(high, chunk), start : start + 128] = sine
+            return carry
+
+        lax.fori_loop(0, waves_each // chunk, some, 0)
+
     factors[...] = jnp.zeros_like(factors)
     gathered[...] = jnp.zeros_like(gathered)
     own_feat.wait()
     norm_scale = 1.0 / math.sqrt(NBR * BLOCK)
 
     def use_shard(origin):
-        phase_step(origin)
         feats = feat_buf[origin].reshape(rows, channels)
         near = rows_of(pos_buf[origin].astype(jnp.float32))
         latent = jnp.dot(feats, fused_w[...], preferred_element_type=jnp.float32)
-        cosine, sine = cos_sin(turns(own_waves, near))
-        phases = jnp.concatenate([cosine, sine], axis=0)
+        phase_rows(origin, near)
         factors[...] += jnp.dot(
-            phases, latent.astype(jnp.bfloat16), preferred_element_type=jnp.float32
+            phase_buf[origin], latent.astype(jnp.bfloat16), preferred_element_type=jnp.float32
         )
         lane_block = lax.broadcasted_iota(jnp.int32, (1, rows), 1) // BLOCK
         for block in range(blocks_here):
@@ -446,6 +465,8 @@
                     weights, feats, preferred_element_type=jnp.float32
                 )
 
+    use_shard(me)
+
     def gather_step(rank, carry):
         @pl.when(rank < lines)
         def _():
@@ -459,26 +480,34 @@
         forward_copy(other).start()
 
         def use_step(which, carry):
-            origin = 2 * shard_line + jnp.where(which == 0, side, 1 - side)
-
-            @pl.when(origin != me)
-            def _():
-                pos_copy(lax.rem(me - origin + n, n)).wait_recv()
-                forward_copy(origin).wait_recv()
-
+            origin = jnp.where(which == 0, 2 * ranked(rank) + side, other)
+            pos_copy(lax.rem(me - origin + n, n)).wait_recv()
+            forward_copy(origin).wait_recv()
             use_shard(origin)
             return carry
 
-        lax.fori_loop(0, 2, use_step, 0)
+        lax.fori_loop(rank // lines, 2, use_step, 0)
         return carry
 
     lax.fori_loop(1, lines + 1, gather_step, 0)
 
     lengths = turns(own_waves, own_waves)
-    gain = jnp.exp(-lengths * rate_ref[...]) * (1.0 / math.sqrt(rows * n))
-    filt_buf[me] = (factors[...] * jnp.concatenate([gain, gain], axis=0)).astype(jnp.bfloat16)
-    send_own(filt_sends, filt_piece(line, side))
-
+    gain = jnp.exp(-lengths * rate_ref[:, tile]) * (1.0 / math.sqrt(rows * n))
+    filt_cols[...] = (factors[...] * jnp.concatenate([gain, gain], axis=0)).T
+    turned = filt_cols[pl.ds(pl.multiple_of(lax.rem(line, per_tile) * part, part), part), :]
+    filt_buf[...] = turned.astype(jnp.bfloat16)
+
+    def sum_of(owner):
+        sums = jnp.dot(filt_buf[...], phase_buf[owner], preferred_element_type=jnp.float32)
+        return (sums * (1.0 / math.sqrt(K))).astype(jnp.bfloat16)
+
+    def sum_step(step, carry):
+        sum_send_buf[peer(step)] = sum_of(peer(step))
+        sum_copy(step).start()
+        return carry
+
+    lax.fori_loop(1, n, sum_step, 0)
+    sum_buf[me] = sum_of(me)
     for load in loads[4:]:
         load.wait()
     short = jnp.zeros(message.shape, jnp.float32)
@@ -489,32 +518,13 @@
             preferred_element_type=jnp.float32,
         )
     message[...] = short
-    summed[...] = jnp.dot(phase_buf[me], filt_buf[me], preferred_element_type=jnp.float32)
-
-    def long_step(rank, carry):
-        @pl.when(rank < lines)
-        def _():
-            pass_on(filt_sends, filt_piece, ranked(rank))
-
-        shard_line = ranked(rank - 1)
-        side_copy(filt_sends, filt_piece(shard_line, 1 - side), shard_line).wait_recv()
-        other = 2 * shard_line + 1 - side
-        summed[...] += jnp.dot(
-            phase_buf[other], filt_buf[other], preferred_element_type=jnp.float32
-        )
-
-        @pl.when(rank < lines)
-        def _():
-            origin = 2 * ranked(rank) + side
-            summed[...] += jnp.dot(
-                phase_buf[origin], filt_buf[origin], preferred_element_type=jnp.float32
-            )
-
-        return carry
-
-    lax.fori_loop(1, lines + 1, long_step, 0)
-
-    reduced = (summed[...] * (1.0 / math.sqrt(K))).astype(jnp.bfloat16)
+    for step in range(1, n):
+        sum_copy(step).wait_recv()
+    for whole in range(lines):
+        summed[whole * part : (whole + 1) * part, :] = sum_buf[2 * whole].astype(
+            jnp.float32
+        ) + sum_buf[2 * whole + 1].astype(jnp.float32)
+    reduced = summed[...].T.astype(jnp.bfloat16)
     width = out_ref.shape[1]
     for target in range(groups):
         low = target * width
@@ -530,10 +540,10 @@
         total += recv_buf[step].astype(jnp.float32)
     out_ref[...] = total.astype(out_ref.dtype)
     finish(feat_sends, feat_piece)
-    finish(filt_sends, filt_piece)
 
     def finish_step(step, carry):
         pos_copy(step).wait_send()
+        sum_copy(step).wait_send()
         forward_copy(peer(step)).wait_send()
         return carry
 
@@ -558,7 +568,8 @@
     groups = lax.axis_size("waves")
     rows, channels = features.shape
     latents = latent_weight.shape[1]
-    waves_each = wavevectors.shape[1] // n
+    waves_each = wavevectors.shape[1] // 2
+    part = latents // (n // 2)
     local_kernels = radial_width.shape[0]
     vmem = pl.BlockSpec(memory_space=pltpu.VMEM)
     held = pl.BlockSpec(memory_space=pl.ANY)
@@ -578,19 +589,23 @@
             pltpu.VMEM(out_weight.shape, jnp.bfloat16),
             pltpu.VMEM((n, 2, rows // 2, channels), jnp.bfloat16),
             pltpu.VMEM((n, 3, rows), jnp.int32),
-            pltpu.VMEM((channels, latents), jnp.bfloat16),
-            pltpu.VMEM((2 * waves_each, latents), jnp.float32),
+            pltpu.VMEM((channels, 128), jnp.bfloat16),
+            pltpu.VMEM((2 * waves_each, 128), jnp.float32),
             pltpu.VMEM((local_kernels, rows, channels), jnp.float32),
-            pltpu.VMEM((n, rows, 2 * waves_each), jnp.bfloat16),
-            pltpu.VMEM((n, 2 * waves_each, latents), jnp.bfloat16),
+            pltpu.VMEM((n, 2 * waves_each, rows), jnp.bfloat16),
+            pltpu.VMEM((3, waves_each, 128), jnp.float32),
+            pltpu.VMEM((128, 2 * waves_each), jnp.float32),
+            pltpu.VMEM((part, 2 * waves_each), jnp.bfloat16),
+            pltpu.VMEM((n, part, rows), jnp.bfloat16),
+            pltpu.VMEM((n, part, rows), jnp.bfloat16),
             pltpu.VMEM((rows, channels), jnp.float32),
-            pltpu.VMEM((rows, latents), jnp.float32),
+            pltpu.VMEM((latents, rows), jnp.float32),
             pltpu.VMEM((groups, rows, channels // groups), jnp.bfloat16),
             pltpu.VMEM((groups, rows, channels // groups), jnp.bfloat16),
             dma((8,)),
             *[dma((n // 2,)) for _ in range(5)],
             *[dma((n,)) for _ in range(4)],
-            *[dma((n // 2,)) for _ in range(5)],
+            *[dma((n,)) for _ in range(2)],
             *[dma((groups,)) for _ in range(2)],
         ],
         compiler_params=pltpu.CompilerParams(
@@ -618,7 +633,10 @@
     reach_hops = -(-REACH // (rows // BLOCK))
     covers_all = 2 * reach_hops + 1 >= n
     if covers_all and groups % 2 == 0 and n % 2 == 0 and rows % (2 * BLOCK) == 0:
-        if wavevectors.shape[1] % (128 * n) == 0:
+        lines = n // 2
+        latents = arrays[6].shape[1]
+        part = latents // lines
+        if wavevectors.shape[1] % 256 == 0 and part in (32, 64, 128) and part * lines == latents:
             return fused(*arrays)
     return local(*arrays)
 

time: 55 us -> 44.8 us (0.81)
  Pallas kernels: 53.4 us -> 43 us
    pallas_call x1, Pallas kernels: 53.4 us -> 43 us  [fused(): pl.pallas_call(functools.partial(fused_kernel, n, groups), out_shape=jax....]
where the time goes in v3:
time: 44.8 us; the launch traced here: 44.5 us
  Pallas kernels  43 us (96%)
  local copies, waits for them, and re-layouts  1.47 us (3%)
    pallas_call x1, Pallas kernels, fused(): pl.pallas_call(functools.partial(fused_kernel, n, groups), out_shape=jax....  43 us
    unnamed x1, local copies, waits for them, and re-layouts  1.47 us

profile of v3, /device:TPU:1, one launch (start us, length us, event | category | flops | bytes accessed | tf_op | source)
XLA Modules:
  0.0 44.5 jit_solution(8395372521084073964)
XLA Ops:
  0.0 43.0 %shard_map.100 = bf16[256,128]{1,0:T(8,128)(2,1)} custom-call(bf16[2,128,512]{2,1,0:T(8,128)(2,1)} %bitcast.2, s32[3,256]{1,0:T(4,128)} %pos_ref.1, s32[2,12]{1,0:T(2,128)} %nbr_ref.1, s32[3,1024]{1,0:T(4,128)} %wave_in.1, f32[2]{0:T(128)} %width_ref.1, bf16[2,512,512]{2,1,0:T(8,128)(2,1)} %short_in.1, bf16[512,256]{1,0:T(8,128)(2,1)} %latw_in.1, ...), custom_call_target="tpu_custom_call" | custom-call | tf_op jit(solution)/shard_map/pallas_call | solution.py:578
  43.0 1.5 %copy.12 = bf16[256,128]{1,0:T(8,128)(2,1)} copy(bf16[256,128]{1,0:T(8,128)(2,1)} %shard_map.100) | data formatting | bytes 131072

commit v4 on v3

--- a/solution.py
+++ b/solution.py
@@ -131,6 +131,7 @@
 
 
 MESH = pl.DeviceIdType.MESH
+PIECES = 4
 SINE = (6.28318516, -41.34165503, 81.60100405, -76.5497817, 39.53670129)
 
 
@@ -222,7 +223,7 @@
     group = lax.axis_index("waves")
     core = lax.rem(group, 2)
     partner = group + 1 - 2 * core
-    half, channels = feat_ref.shape[1], feat_ref.shape[2]
+    half, channels = feat_ref.shape[1] * feat_ref.shape[2], feat_ref.shape[3]
     rows = 2 * half
     blocks_here = rows // BLOCK
     local_kernels = short_ref.shape[0]
@@ -246,72 +247,78 @@
         far_line = jnp.where(line < lines - 1 - line, rank, lines - 1 - rank)
         return jnp.where(rank <= 2 * closest, near_line, far_line)
 
-    def line_copy(sends, piece, shard_line, direction):
+    def line_copy(sends, piece, slot, direction):
         up_send, down_send, line_recv, _, _ = sends
         return pltpu.make_async_remote_copy(
             src_ref=piece[0],
             dst_ref=piece[1],
-            send_sem=(up_send if direction > 0 else down_send).at[shard_line],
-            recv_sem=line_recv.at[shard_line],
+            send_sem=(up_send if direction > 0 else down_send).at[slot],
+            recv_sem=line_recv.at[slot],
             device_id={"atoms": me + 2 * direction},
             device_id_type=MESH,
         )
 
-    def side_copy(sends, piece, shard_line):
+    def side_copy(sends, piece, slot):
         return pltpu.make_async_remote_copy(
             src_ref=piece[0],
             dst_ref=piece[1],
-            send_sem=sends[3].at[shard_line],
-            recv_sem=sends[4].at[shard_line],
+            send_sem=sends[3].at[slot],
+            recv_sem=sends[4].at[slot],
             device_id={"atoms": me + 1 - 2 * side},
             device_id_type=MESH,
         )
 
-    def feat_piece(shard_line, shard_side):
-        place = feat_buf.at[2 * shard_line + shard_side, core]
+    def feat_piece(shard_line, shard_side, which):
+        place = feat_buf.at[2 * shard_line + shard_side, core, which]
         return place, place
 
-    def send_own(sends, piece):
+    def send_own(sends, which):
+        piece = (feat_ref.at[core, which], feat_buf.at[me, core, which])
+        slot = line * PIECES + which
+
         @pl.when(line < lines - 1)
         def _():
-            line_copy(sends, piece, line, 1).start()
+            line_copy(sends, piece, slot, 1).start()
 
         @pl.when(line > 0)
         def _():
-            line_copy(sends, piece, line, -1).start()
-
-        side_copy(sends, piece, line).start()
-
-    def pass_on(sends, piece_of, shard_line):
-        piece = piece_of(shard_line, side)
-        line_copy(sends, piece, shard_line, 1).wait_recv()
+            line_copy(sends, piece, slot, -1).start()
+
+        side_copy(sends, piece, slot).start()
+
+    def pass_on(sends, shard_line, which):
+        piece = feat_piece(shard_line, side, which)
+        slot = shard_line * PIECES + which
+        line_copy(sends, piece, slot, 1).wait_recv()
 
         @pl.when((shard_line < line) & (line < lines - 1))
         def _():
-            line_copy(sends, piece, shard_line, 1).start()
+            line_copy(sends, piece, slot, 1).start()
 
         @pl.when((shard_line > line) & (line > 0))
         def _():
-            line_copy(sends, piece, shard_line, -1).start()
-
-        side_copy(sends, piece, shard_line).start()
-
-    def finish(sends, piece_of):
-        def one(shard_line, carry):
-            piece = piece_of(shard_line, side)
+            line_copy(sends, piece, slot, -1).start()
+
+        side_copy(sends, piece, slot).start()
+        forward_copy(2 * shard_line + side, which).start()
+
+    def finish(sends):
+        def one(slot, carry):
+            shard_line = slot // PIECES
+            piece = feat_piece(shard_line, side, lax.rem(slot, PIECES))
 
             @pl.when((shard_line <= line) & (line < lines - 1))
             def _():
-                line_copy(sends, piece, shard_line, 1).wait_send()
+                line_copy(sends, piece, slot, 1).wait_send()
 
             @pl.when((shard_line >= line) & (line > 0))
             def _():
-                line_copy(sends, piece, shard_line, -1).wait_send()
-
-            side_copy(sends, piece, shard_line).wait_send()
+                line_copy(sends, piece, slot, -1).wait_send()
+
+            side_copy(sends, piece, slot).wait_send()
             return carry
 
-        lax.fori_loop(0, lines, one, 0)
+        lax.fori_loop(0, lines * PIECES, one, 0)
 
     def pos_copy(step):
         return pltpu.make_async_remote_copy(
@@ -323,12 +330,12 @@
             device_id_type=MESH,
         )
 
-    def forward_copy(origin):
+    def forward_copy(origin, which):
         return pltpu.make_async_remote_copy(
-            src_ref=feat_buf.at[origin, core],
-            dst_ref=feat_buf.at[origin, core],
-            send_sem=fwd_send.at[origin],
-            recv_sem=fwd_recv.at[origin],
+            src_ref=feat_buf.at[origin, core, which],
+            dst_ref=feat_buf.at[origin, core, which],
+            send_sem=fwd_send.at[origin * PIECES + which],
+            recv_sem=fwd_recv.at[origin * PIECES + which],
             device_id={"waves": partner},
             device_id_type=MESH,
         )
@@ -388,7 +395,8 @@
         )
     pl.semaphore_wait(barrier, n - 1 + groups - 1)
 
-    send_own(feat_sends, (feat_ref.at[core], feat_buf.at[me, core]))
+    for which in range(PIECES):
+        send_own(feat_sends, which)
     for step in range(1, n):
         pos_copy(step).start()
 
@@ -467,29 +475,45 @@
 
     use_shard(me)
 
+    def take(origin):
+        pos_copy(lax.rem(me - origin + n, n)).wait_recv()
+        for which in range(PIECES):
+            forward_copy(origin, which).wait_recv()
+        use_shard(origin)
+
     def gather_step(rank, carry):
-        @pl.when(rank < lines)
-        def _():
-            shard_line = ranked(rank)
-            pass_on(feat_sends, feat_piece, shard_line)
-            forward_copy(2 * shard_line + side).start()
-
-        shard_line = ranked(rank - 1)
-        other = 2 * shard_line + 1 - side
-        side_copy(feat_sends, feat_piece(shard_line, 1 - side), shard_line).wait_recv()
-        forward_copy(other).start()
-
-        def use_step(which, carry):
-            origin = jnp.where(which == 0, 2 * ranked(rank) + side, other)
-            pos_copy(lax.rem(me - origin + n, n)).wait_recv()
-            forward_copy(origin).wait_recv()
-            use_shard(origin)
-            return carry
-
-        lax.fori_loop(rank // lines, 2, use_step, 0)
+        def stage(turn, inner):
+            @pl.when(rank < lines)
+            def _():
+                for which in range(PIECES // 2):
+                    pass_on(feat_sends, ranked(rank), turn * (PIECES // 2) + which)
+
+            before = ranked(rank - 1)
+            after = ranked(jnp.maximum(rank - 2, 0))
+
+            @pl.when((turn == 1) & (rank <= lines))
+            def _():
+                for which in range(PIECES):
+                    side_copy(
+                        feat_sends,
+                        feat_piece(before, 1 - side, which),
+                        before * PIECES + which,
+                    ).wait_recv()
+                    forward_copy(2 * before + 1 - side, which).start()
+
+            use_now = jnp.where(turn == 0, rank >= 2, (rank >= 2) & (rank <= lines))
+            origin = jnp.where(turn == 0, 2 * after + 1 - side, 2 * before + side)
+
+            @pl.when(use_now)
+            def _():
+                take(origin)
+
+            return inner
+
+        lax.fori_loop(0, jnp.where(rank <= lines, 2, 1), stage, 0)
         return carry
 
-    lax.fori_loop(1, lines + 1, gather_step, 0)
+    lax.fori_loop(1, lines + 2, gather_step, 0)
 
     lengths = turns(own_waves, own_waves)
     gain = jnp.exp(-lengths * rate_ref[:, tile]) * (1.0 / math.sqrt(rows * n))
@@ -539,12 +563,13 @@
         msg_copy(step).wait_recv()
         total += recv_buf[step].astype(jnp.float32)
     out_ref[...] = total.astype(out_ref.dtype)
-    finish(feat_sends, feat_piece)
+    finish(feat_sends)
 
     def finish_step(step, carry):
         pos_copy(step).wait_send()
         sum_copy(step).wait_send()
-        forward_copy(peer(step)).wait_send()
+        for which in range(PIECES):
+            forward_copy(peer(step), which).wait_send()
         return carry
 
     lax.fori_loop(1, n, finish_step, 0)
@@ -587,7 +612,7 @@
             pltpu.VMEM(mix_weight.shape, jnp.float32),
             pltpu.VMEM((1, latents), jnp.float32),
             pltpu.VMEM(out_weight.shape, jnp.bfloat16),
-            pltpu.VMEM((n, 2, rows // 2, channels), jnp.bfloat16),
+            pltpu.VMEM((n, 2, PIECES, rows // 2 // PIECES, channels), jnp.bfloat16),
             pltpu.VMEM((n, 3, rows), jnp.int32),
             pltpu.VMEM((channels, 128), jnp.bfloat16),
             pltpu.VMEM((2 * waves_each, 128), jnp.float32),
@@ -603,8 +628,9 @@
             pltpu.VMEM((groups, rows, channels // groups), jnp.bfloat16),
             pltpu.VMEM((groups, rows, channels // groups), jnp.bfloat16),
             dma((8,)),
-            *[dma((n // 2,)) for _ in range(5)],
-            *[dma((n,)) for _ in range(4)],
+            *[dma((n // 2 * PIECES,)) for _ in range(5)],
+            *[dma((n,)) for _ in range(2)],
+            *[dma((n * PIECES,)) for _ in range(2)],
             *[dma((n,)) for _ in range(2)],
             *[dma((groups,)) for _ in range(2)],
         ],
@@ -612,7 +638,7 @@
             collective_id=0, has_side_effects=True, vmem_limit_bytes=67043328
         ),
     )(
-        features.reshape(2, rows // 2, channels),
+        features.reshape(2, PIECES, rows // 2 // PIECES, channels),
         positions,
         neighbours,
         wavevectors,

time: 44.8 us -> 41.9 us (0.935)
  Pallas kernels: 43 us -> 40.2 us
    pallas_call x1, Pallas kernels: 43 us -> 40.2 us  [fused(): pl.pallas_call(functools.partial(fused_kernel, n, groups), out_shape=jax....]
where the time goes in v4:
time: 41.9 us; the launch traced here: 41.7 us
  Pallas kernels  40.2 us (96%)
  local copies, waits for them, and re-layouts  1.47 us (4%)
    pallas_call x1, Pallas kernels, fused(): pl.pallas_call(functools.partial(fused_kernel, n, groups), out_shape=jax....  40.2 us
    unnamed x1, local copies, waits for them, and re-layouts  1.47 us

profile of v4, /device:TPU:1, one launch (start us, length us, event | category | flops | bytes accessed | tf_op | source)
XLA Modules:
  0.0 41.7 jit_solution(15906198156718083093)
XLA Ops:
  0.0 40.2 %shard_map.100 = bf16[256,128]{1,0:T(8,128)(2,1)} custom-call(bf16[2,4,32,512]{3,2,1,0:T(8,128)(2,1)} %bitcast.2, s32[3,256]{1,0:T(4,128)} %pos_ref.1, s32[2,12]{1,0:T(2,128)} %nbr_ref.1, s32[3,1024]{1,0:T(4,128)} %wave_in.1, f32[2]{0:T(128)} %width_ref.1, bf16[2,512,512]{2,1,0:T(8,128)(2,1)} %short_in.1, bf16[512,256]{1,0:T(8,128)(2,1)} %latw_in.1, ...), custom_call_target="tpu_custom_call" | custom-call | tf_op jit(solution)/shard_map/pallas_call | solution.py:603
  40.2 1.5 %copy.12 = bf16[256,128]{1,0:T(8,128)(2,1)} copy(bf16[256,128]{1,0:T(8,128)(2,1)} %shard_map.100) | data formatting | bytes 131072

commit v5 on v4

--- a/solution.py
+++ b/solution.py
@@ -550,15 +550,18 @@
         ) + sum_buf[2 * whole + 1].astype(jnp.float32)
     reduced = summed[...].T.astype(jnp.bfloat16)
     width = out_ref.shape[1]
-    for target in range(groups):
-        low = target * width
-        part = message[:, low : low + width] + jnp.dot(
-            reduced, outw_ref[:, low : low + width], preferred_element_type=jnp.float32
-        )
-        send_buf[target] = part.astype(jnp.bfloat16)
-    for step in range(1, groups):
-        msg_copy(step).start()
-    total = send_buf[group].astype(jnp.float32)
+    order = sorted(range(1, groups), key=lambda step: abs(step - groups // 2))
+    for step in [*order, 0]:
+        target = lax.rem(group + step, groups)
+        columns = pl.ds(pl.multiple_of(target * width, width), width)
+        part_sum = message[:, columns] + jnp.dot(
+            reduced, outw_ref[:, columns], preferred_element_type=jnp.float32
+        )
+        if step == 0:
+            total = part_sum
+        else:
+            send_buf[target] = part_sum.astype(jnp.bfloat16)
+            msg_copy(step).start()
     for step in range(1, groups):
         msg_copy(step).wait_recv()
         total += recv_buf[step].astype(jnp.float32)

time: 41.9 us -> 41.7 us (level)
  no operation moved by 1% of the time
where the time goes in v5:
time: 41.7 us; the launch traced here: 41.6 us
  Pallas kernels  40.1 us (96%)
  local copies, waits for them, and re-layouts  1.47 us (4%)
    pallas_call x1, Pallas kernels, fused(): pl.pallas_call(functools.partial(fused_kernel, n, groups), out_shape=jax....  40.1 us
    unnamed x1, local copies, waits for them, and re-layouts  1.47 us

profile of v5, /device:TPU:1, one launch (start us, length us, event | category | flops | bytes accessed | tf_op | source)
XLA Modules:
  0.0 41.6 jit_solution(1974835457961578363)
XLA Ops:
  0.0 40.1 %shard_map.100 = bf16[256,128]{1,0:T(8,128)(2,1)} custom-call(bf16[2,4,32,512]{3,2,1,0:T(8,128)(2,1)} %bitcast.2, s32[3,256]{1,0:T(4,128)} %pos_ref.1, s32[2,12]{1,0:T(2,128)} %nbr_ref.1, s32[3,1024]{1,0:T(4,128)} %wave_in.1, f32[2]{0:T(128)} %width_ref.1, bf16[2,512,512]{2,1,0:T(8,128)(2,1)} %short_in.1, bf16[512,256]{1,0:T(8,128)(2,1)} %latw_in.1, ...), custom_call_target="tpu_custom_call" | custom-call | tf_op jit(solution)/shard_map/pallas_call | solution.py:606
  40.1 1.5 %copy.12 = bf16[256,128]{1,0:T(8,128)(2,1)} copy(bf16[256,128]{1,0:T(8,128)(2,1)} %shard_map.100) | data formatting | bytes 131072
